TPU v7x, 32 devices: a whole 2x2x4 slice. The times are simulated.
32 devices in a mesh: mode: 8 (over z, x), row: 4 (over y, core).
Axes of the slice: x: 2, y: 2, z: 4, core: 2. Of those that a mesh axis runs over, the one named last changes fastest.
Arguments:
- forward: bfloat16 [64, 8, 2, 512], P('mode', 'row'), may hold values from -6 to 6
- backward: bfloat16 [64, 8, 2, 512], P('mode', 'row'), may hold values from -6 to 6
- propagator: bfloat16 [2, 512, 512], replicated, may hold values from -0.1875 to 0.1875
- row_taps: float32 [2, 3], replicated, may hold values from -3 to 3
- phase_masks: float32 [7, 8, 512], P(None, 'row'), may hold values from -3.140625 to 3.140625
- plane_index: int32 [4], replicated, may hold values from 0 to 6
- wave_ratio: float32 [4], replicated, may hold values from 0.7 to 1.4
- pair_list: int32 [80, 2], replicated, may hold values from 0 to 15, as said below
Outputs:
- coupling: float32 [2, 64, 64], P(None, 'mode')
- mask_grad: float32 [4, 8, 512], P(None, 'row')
Inputs may be any that keep to these rules, and one draw needn't show every extreme that they name: `pair_list`: each row names a target group and a forward group; no pair appears twice and every group is paired with itself; 80 pairs in all.
All inputs are finite; a program needn't handle non-finite values.
Results may differ from a plain program's by a relative error of at most 0.0078.
Values may be sent and summed in bfloat16 or wider, within the bound.
No kernel may reach another device: no remote copies, remote signals or barrier semaphores. Data moves between devices by JAX's collectives and lax.ppermute only.
A program may use at most 64 MiB of HBM per device.

v0:
```python
import math
import jax
import jax.numpy as jnp
from jax import lax
from jax.sharding import PartitionSpec as P

NG = 16


def padded_2(array, sides, width):
    for axis, dim in sides:
        peers, length = (lax.axis_size(axis), array.shape[dim])
        up = [(i, (i + 1) % peers) for i in range(peers - 1)]
        down = [(j, i) for i, j in up]
        last = lax.slice_in_dim(array, length - width, length, axis=dim)
        leading = lax.slice_in_dim(array, 0, width, axis=dim)
        before = lax.ppermute(last, axis, up)
        after = lax.ppermute(leading, axis, down)
        array = jnp.concatenate([before, array, after], axis=dim)
    return array


def chosen_phases(phase_masks, plane_index, wave_ratio):
    planes = jnp.arange(phase_masks.shape[0], dtype=jnp.int32)
    selector = (plane_index[:, None] == planes[None, :]).astype(jnp.float32)
    picked = jnp.einsum("wp,prc->wrc", selector, phase_masks, precision=lax.Precision.HIGHEST)
    return picked * wave_ratio[:, None, None]


def apply_mask(forward, phases):
    mode_total, row_total, _, width = forward.shape
    wave_total = phases.shape[0]
    shaped = forward.astype(jnp.float32).reshape(
        mode_total // wave_total, wave_total, row_total, 2, width
    )
    cosine = jnp.cos(phases)[None]
    sine = jnp.sin(phases)[None]
    real_part = shaped[:, :, :, 0] * cosine - shaped[:, :, :, 1] * sine
    imag_part = shaped[:, :, :, 0] * sine + shaped[:, :, :, 1] * cosine
    return jnp.stack([real_part, imag_part], axis=3).reshape(forward.shape).astype(jnp.bfloat16)


def forward_matrix(propagator):
    top_half = jnp.concatenate([propagator[0], propagator[1]], axis=1)
    low_half = jnp.concatenate([-propagator[1], propagator[0]], axis=1)
    return jnp.concatenate([top_half, low_half], axis=0)


def backward_matrix(propagator):
    top_half = jnp.concatenate([propagator[0].T, -propagator[1].T], axis=1)
    low_half = jnp.concatenate([propagator[1].T, propagator[0].T], axis=1)
    return jnp.concatenate([top_half, low_half], axis=0)


def propagate(fields, matrix):
    width = fields.shape[-1]
    result = jnp.dot(fields.reshape(-1, 2 * width), matrix, preferred_element_type=jnp.float32)
    return result.reshape(fields.shape)


def row_stencil(padded, row_taps, adjoint):
    values = padded.astype(jnp.float32)
    below_rows = values[:, :-2]
    center = values[:, 1:-1]
    above_rows = values[:, 2:]
    tap_real = row_taps[0]
    tap_imag = row_taps[1]
    if adjoint:
        sources = (above_rows, center, below_rows)
        tap_imag = -tap_imag
    else:
        sources = (below_rows, center, above_rows)
    real_sum = jnp.zeros(center[:, :, 0].shape, jnp.float32)
    imag_sum = jnp.zeros(center[:, :, 0].shape, jnp.float32)
    for position in range(3):
        source = sources[position]
        real_sum = (
            real_sum + tap_real[position] * source[:, :, 0] - tap_imag[position] * source[:, :, 1]
        )
        imag_sum = (
            imag_sum + tap_real[position] * source[:, :, 1] + tap_imag[position] * source[:, :, 0]
        )
    return jnp.stack([real_sum, imag_sum], axis=2)


def times_i(fields):
    return jnp.stack([-fields[:, :, 1], fields[:, :, 0]], axis=2)


def times_minus_i(fields):
    return jnp.stack([fields[:, :, 1], -fields[:, :, 0]], axis=2)


def body(forward, backward, propagator, row_taps, phase_masks, plane_index, wave_ratio, pair_list):
    local_modes, local_rows, _, width = forward.shape
    wave_total = wave_ratio.shape[0]
    mode_total = local_modes * lax.axis_size("mode")
    row_total = local_rows * lax.axis_size("row")
    group_size = mode_total // NG
    phases = chosen_phases(phase_masks, plane_index, wave_ratio)
    masked = apply_mask(forward, phases)
    spread = propagate(masked, forward_matrix(propagator)).astype(jnp.bfloat16)
    padded = padded_2(spread, (("row", 1),), 1)
    field = row_stencil(padded, row_taps, False).astype(jnp.bfloat16)
    field_flat = field.reshape(local_modes, -1)
    field_turned = times_minus_i(field).reshape(local_modes, -1)
    group_ids = jnp.arange(NG, dtype=jnp.int32)
    hits = (pair_list[:, 0][:, None, None] == group_ids[None, :, None]) & (
        pair_list[:, 1][:, None, None] == group_ids[None, None, :]
    )
    pair_matrix = jnp.sum(hits.astype(jnp.float32), axis=0)
    own_modes = lax.axis_index("mode") * local_modes + jnp.arange(local_modes, dtype=jnp.int32)
    own_onehot = ((own_modes // group_size)[:, None] == group_ids[None, :]).astype(jnp.float32)
    target_groups = jnp.arange(mode_total, dtype=jnp.int32) // group_size
    target_onehot = (target_groups[:, None] == group_ids[None, :]).astype(jnp.float32)
    own_pairs = jnp.dot(own_onehot, pair_matrix.T, precision=lax.Precision.HIGHEST)
    column_mask = jnp.dot(own_pairs, target_onehot.T, precision=lax.Precision.HIGHEST)
    shard_rows = lax.all_gather(backward, "mode", axis=0, tiled=True)
    rows_flat = shard_rows.reshape(shard_rows.shape[0], -1)
    real_part = jnp.einsum("nd,kd->nk", field_flat, rows_flat, preferred_element_type=jnp.float32)
    imag_part = jnp.einsum("nd,kd->nk", field_turned, rows_flat, preferred_element_type=jnp.float32)
    block = jnp.stack([real_part, imag_part])
    match_sum = lax.psum(block, "row")
    coupling = match_sum * (1.0 / math.sqrt(row_total * width)) * column_mask[None, :, :]
    weights = coupling.astype(jnp.bfloat16)
    shard_rows = lax.all_gather(backward, "mode", axis=0, tiled=True)
    row_count = shard_rows.shape[0]
    rows_flat = shard_rows.reshape(row_count, -1)
    rows_turned = times_i(shard_rows).reshape(row_count, -1)
    weight_real = weights[0]
    weight_imag = weights[1]
    running = jnp.dot(weight_real, rows_flat, preferred_element_type=jnp.float32)
    gathered = running + jnp.dot(weight_imag, rows_turned, preferred_element_type=jnp.float32)
    gathered = (
        (gathered * (1.0 / math.sqrt(mode_total))).astype(jnp.bfloat16).reshape(forward.shape)
    )
    padded_back = padded_2(gathered, (("row", 1),), 1)
    pulled = row_stencil(padded_back, row_taps, True).astype(jnp.bfloat16)
    adjoint = propagate(pulled, backward_matrix(propagator))
    masked_float = masked.astype(jnp.float32)
    term = masked_float[:, :, 1] * adjoint[:, :, 0] - masked_float[:, :, 0] * adjoint[:, :, 1]
    partial_grad = jnp.sum(
        term.reshape(local_modes // wave_total, wave_total, local_rows, width), axis=0
    )
    summed = lax.psum(partial_grad, "mode")
    mask_grad = summed * (-2.0 / math.sqrt(mode_total))
    return (coupling, mask_grad)


def solution(mesh):
    in_specs = (
        P("mode", "row", None, None),
        P("mode", "row", None, None),
        P(),
        P(),
        P(None, "row", None),
        P(),
        P(),
        P(),
    )
    out_specs = (P(None, "mode", None), P(None, "row", None))
    return jax.shard_map(body, mesh=mesh, in_specs=in_specs, out_specs=out_specs, check_vma=False)
```

profile of v0, /device:TPU:0, one launch (start us, length us, event | category | flops | bytes accessed | tf_op | source)
XLA Modules:
  0.0 117.6 jit_solution(7645582533571077190)
XLA Ops:
  0.6 0.0 copy-start
  0.6 0.0 copy-start.1
  0.7 0.0 copy-start.2
  0.7 0.0 copy-start.7
  0.7 0.0 copy-start.6
  0.7 2.7 %slice_bitcast_fusion = (bf16[512,512]{0,1:T(8,128)(2,1)}, bf16[512,512]{0,1:T(8,128)(2,1)}, bf16[512,512]{1,0:T(8,128)(2,1)}, bf16[512,512]{1,0:T(8,128)(2,1)}) fusion(bf16[2,512,512]{2,1,0:T(8,128)(2,1)} %param.10), kind=kLoop, calls=%fused_computation.10 | loop fusion | bytes 3145728 | tf_op jit(solution)/shard_map/transpose | solution.py:50
  3.4 0.0 copy-done.1
  3.4 0.9 fusion.19
  4.3 0.0 copy-done
  4.4 0.0 copy-done.7
  4.4 0.0 copy-done.6
  4.4 0.3 fusion.26
  4.8 1.8 %maximum_bitcast_fusion = bf16[1024,1024]{0,1:T(8,128)(2,1)S(1)} fusion(bf16[512,512]{1,0:T(8,128)(2,1)} %get-tuple-element.13, bf16[512,512]{1,0:T(8,128)(2,1)} %fusion.19, bf16[512,512]{1,0:T(8,128)(2,1)} %get-tuple-element.12), kind=kLoop, calls=%fused_computation.3 | loop fusion | flops 8388608 | bytes 3670016 | tf_op jit(solution)/shard_map/dot_general | solution.py:57
  6.6 2.6 %copy.33 = bf16[1024,1024]{1,0:T(8,128)(2,1)} copy(bf16[1024,1024]{0,1:T(8,128)(2,1)S(1)} %maximum_bitcast_fusion) | data formatting | bytes 4194304 | tf_op jit(solution)/shard_map/dot_general | solution.py:57
  9.2 2.3 %convolution_convert_fusion = bf16[8,2,2,512]{3,0,2,1:T(8,128)(2,1)S(1)} fusion(bf16[8,2,1024,1]{2,0,3,1:T(8,128)(2,1)S(1)} %bitcast.95, bf16[2,512,1024,1]{2,1,0,3:T(8,128)(2,1)} %bitcast.92), kind=kOutput, calls=%fused_computation.5 | convolution fusion | flops 33570816 | bytes 2162688 | tf_op jit(solution)/shard_map/dot_general | solution.py:57
  11.5 2.4 %collective-permute-start = (bf16[8,1,2,512]{3,0,2,1:T(8,128)(2,1)S(1)}, bf16[8,1,2,512]{3,0,2,1:T(8,128)(2,1)S(1)}, u32[]{:S(2)}, u32[]{:S(2)}) collective-permute-start(bf16[8,1,2,512]{3,0,2,1:T(8,128)(2,1)S(1)} %get-tuple-element.22), channel_id=1, source_target_pairs={{0,1},{1,2},{2,3},{4,5},{5,6},{6,7},{8,9},{9,10},{10,11},{12,13},{... | collective-permute-start | bytes 49160 | tf_op jit(solution)/shard_map/ppermute | solution.py:17
  13.9 1.3 %collective-permute-start.1 = (bf16[8,1,2,512]{3,0,2,1:T(8,128)(2,1)S(1)}, bf16[8,1,2,512]{3,0,2,1:T(8,128)(2,1)S(1)}, u32[]{:S(2)}, u32[]{:S(2)}) collective-permute-start(bf16[8,1,2,512]{3,0,2,1:T(8,128)(2,1)S(1)} %get-tuple-element.23), channel_id=1, source_target_pairs={{1,0},{2,1},{3,2},{5,4},{6,5},{7,6},{9,8},{10,9},{11,10},{13,12},{... | collective-permute-start | bytes 49160 | tf_op jit(solution)/shard_map/ppermute | solution.py:18
  15.2 0.8 fusion.20
  16.0 31.9 %all_gather.4 = bf16[64,2,2,512]{3,0,2,1:T(8,128)(2,1)S(1)} all-gather(bf16[8,2,2,512]{3,0,2,1:T(8,128)(2,1)S(1)} %copy.34), channel_id=1, replica_groups=mesh['mode'=8,'row'=4] {'mode'}, dimensions={0}, use_global_device_ids=true | all-gather | bytes 294912 | tf_op jit(solution)/shard_map/all_gather | solution.py:118
  48.0 0.1 convert_reduce_fusion
  48.1 0.2 fusion.11
  48.3 0.2 convolution_multiply_fusion.1
  48.5 0.1 pad_maximum_fusion
  48.6 1.8 %maximum_maximum_fusion = bf16[1024,1024]{0,1:T(8,128)(2,1)S(1)} fusion(bf16[512,512]{0,1:T(8,128)(2,1)} %get-tuple-element.11, bf16[512,512]{0,1:T(8,128)(2,1)} %get-tuple-element.10, bf16[512,512]{0,1:T(8,128)(2,1)} %fusion.20), kind=kLoop, calls=%fused_computation.4 | loop fusion | flops 8388608 | bytes 3670016 | tf_op jit(solution)/shard_map/concatenate | solution.py:52
  50.4 0.7 fusion.27
  51.0 0.3 copy.35
  51.3 0.2 reshape.169
  51.5 0.3 copy.36
  51.8 0.2 reshape.170
  52.0 0.0 collective-permute-done
  52.0 0.0 collective-permute-done.1
  52.0 3.7 %fusion.22 = (bf16[8,2,1,512]{3,0,2,1:T(8,128)(2,1)S(1)}, bf16[8,2,1,512]{3,0,2,1:T(8,128)(2,1)S(1)}) fusion(f32[8,4,2,512]{3,0,2,1:T(8,128)S(1)} %maximum_convert_fusion, f32[]{:T(128)} %bitcast.16, f32[]{:T(128)} %bitcast.15, f32[]{:T(128)} %bitcast.14, f32[]{:T(128)} %bitcast.13, f32[]{:T(128)} %bitcast.12, f32[]{:T(128)} %bitcast), kind=kLoop, calls=%fused_computation.70 | loop fusion | flops 106496 | bytes 229400 | tf_op jit(solution)/shard_map/neg | solution.py:91
  55.7 3.7 %add_convert_fusion.1 = bf16[8,2,1,512]{3,0,2,1:T(8,128)(2,1)S(1)} fusion(f32[8,4,2,512]{3,0,2,1:T(8,128)S(1)} %maximum_convert_fusion, f32[]{:T(128)} %bitcast.16, f32[]{:T(128)} %bitcast.15, f32[]{:T(128)} %bitcast.14, f32[]{:T(128)} %bitcast.13, f32[]{:T(128)} %bitcast.12, f32[]{:T(128)} %bitcast), kind=kLoop, calls=%fused_computation.33 | loop fusion | flops 98304 | bytes 213016 | tf_op jit(solution)/shard_map/slice | solution.py:91
  59.5 0.2 convolution_bitcast_fusion.1
  59.7 0.2 convolution_bitcast_fusion
  59.8 7.7 %psum.14 = f32[2,8,64]{2,1,0:T(8,128)S(1)} all-reduce(f32[2,8,64]{2,1,0:T(8,128)S(1)} %pad_maximum_fusion.2), channel_id=1, replica_groups=mesh['mode'=8,'row'=4] {'row'}, use_global_device_ids=true, to_apply=%region_0.0 | all-reduce | flops 1024 | bytes 8192 | tf_op jit(solution)/shard_map/psum | solution.py:123
  67.6 0.6 fusion.21
  68.2 0.1 fusion.12
  68.3 0.2 fusion.1
  68.5 2.3 %collective-permute-start.2 = (bf16[8,1,2,512]{3,0,2,1:T(8,128)(2,1)S(1)}, bf16[8,1,2,512]{3,0,2,1:T(8,128)(2,1)S(1)}, u32[]{:S(2)}, u32[]{:S(2)}) collective-permute-start(bf16[8,1,2,512]{3,0,2,1:T(8,128)(2,1)S(1)} %get-tuple-element.20), channel_id=1, source_target_pairs={{0,1},{1,2},{2,3},{4,5},{5,6},{6,7},{8,9},{9,10},{10,11},{12,13},{... | collective-permute-start | bytes 49160 | tf_op jit(solution)/shard_map/ppermute | solution.py:17
  70.8 1.3 %collective-permute-start.3 = (bf16[8,1,2,512]{3,0,2,1:T(8,128)(2,1)S(1)}, bf16[8,1,2,512]{3,0,2,1:T(8,128)(2,1)S(1)}, u32[]{:S(2)}, u32[]{:S(2)}) collective-permute-start(bf16[8,1,2,512]{3,0,2,1:T(8,128)(2,1)S(1)} %get-tuple-element.21), channel_id=1, source_target_pairs={{1,0},{2,1},{3,2},{5,4},{6,5},{7,6},{9,8},{10,9},{11,10},{13,12},{... | collective-permute-start | bytes 49160 | tf_op jit(solution)/shard_map/ppermute | solution.py:18
  72.1 0.7 fusion.28
  72.8 0.0 collective-permute-done.2
  72.8 2.6 %collective-permute-done.3 = bf16[8,1,2,512]{3,0,2,1:T(8,128)(2,1)S(1)} collective-permute-done((bf16[8,1,2,512]{3,0,2,1:T(8,128)(2,1)S(1)}, bf16[8,1,2,512]{3,0,2,1:T(8,128)(2,1)S(1)}, u32[]{:S(2)}, u32[]{:S(2)}) %collective-permute-start.3) | collective-permute-done | bytes 16416 | tf_op jit(solution)/shard_map/ppermute | solution.py:18
  75.4 3.8 %subtract_convert_fusion = (bf16[8,2,1,512]{3,0,2,1:T(8,128)(2,1)S(1)}, bf16[8,2,1,512]{3,0,2,1:T(8,128)(2,1)S(1)}) fusion(f32[8,4,2,512]{3,0,2,1:T(8,128)S(1)} %maximum_convert_fusion.1, f32[]{:T(128)} %bitcast.30, f32[]{:T(128)} %bitcast.29, f32[]{:T(128)} %bitcast.28, f32[]{:T(128)} %bitcast.15, f32[]{:T(128)} %bitcast.13, f32[]{:T(128)} %bitcast), kind=kLoop, calls=%fused_computation.31 | loop fusion | flops 196608 | bytes 229400 | tf_op jit(solution)/shard_map/convert.1
  79.2 0.6 fusion.29
  79.9 37.1 %psum.15 = f32[4,2,512]{2,0,1:T(4,128)S(1)} all-reduce(f32[4,2,512]{2,0,1:T(4,128)S(1)} %reduce_sum.19), channel_id=1, replica_groups=mesh['mode'=8,'row'=4] {'mode'}, use_global_device_ids=true, to_apply=%region_3.4 | all-reduce | flops 4096 | bytes 32768 | tf_op jit(solution)/shard_map/psum | solution.py:145
  117.0 0.6 copy.37
  (31 shorter events, 0.3 us)
Async XLA Ops:
  0.6 3.7 %copy-start = (f32[7,2,512]{2,1,0:T(2,128)S(1)}, f32[7,2,512]{2,1,0:T(2,128)}, u32[]{:S(2)}) copy-start(f32[7,2,512]{2,1,0:T(2,128)} %param.12) | copy-start | bytes 86020
  0.6 2.8 %copy-start.1 = (bf16[2,512,512]{2,1,0:T(8,128)(2,1)S(1)}, bf16[2,512,512]{2,1,0:T(8,128)(2,1)}, u32[]{:S(2)}) copy-start(bf16[2,512,512]{2,1,0:T(8,128)(2,1)} %param.10) | copy-start | bytes 3145732
  0.7 3.6 %copy-start.2 = (bf16[8,2,2,512]{3,2,1,0:T(2,128)(2,1)S(1)}, bf16[8,2,2,512]{3,2,1,0:T(2,128)(2,1)}, u32[]{:S(2)}) copy-start(bf16[8,2,2,512]{3,2,1,0:T(2,128)(2,1)} %param.8) | copy-start | bytes 98308
  0.7 3.7 %copy-start.7 = (s32[4]{0:T(128)S(1)}, s32[4]{0:T(128)}, u32[]{:S(2)}) copy-start(s32[4]{0:T(128)} %param.13) | copy-start | bytes 52
  0.7 3.7 %copy-start.6 = (f32[4]{0:T(128)S(1)}, f32[4]{0:T(128)}, u32[]{:S(2)}) copy-start(f32[4]{0:T(128)} %param.14) | copy-start | bytes 52
  9.2 6.8 %copy-start.3 = (bf16[8,2,2,512]{3,2,1,0:T(2,128)(2,1)S(1)}, bf16[8,2,2,512]{3,2,1,0:T(2,128)(2,1)}, u32[]{:S(2)}) copy-start(bf16[8,2,2,512]{3,2,1,0:T(2,128)(2,1)} %param.9) | copy-start | bytes 98308
  9.2 38.7 %copy-start.5 = (s32[80,2]{0,1:T(2,128)S(1)}, s32[80,2]{0,1:T(2,128)}, u32[]{:S(2)}) copy-start(s32[80,2]{0,1:T(2,128)} %param.15) | copy-start | bytes 1924
  9.2 38.8 %copy-start.4 = (f32[2,3]{1,0:T(2,128)S(1)}, f32[2,3]{1,0:T(2,128)}, u32[]{:S(2)}) copy-start(f32[2,3]{1,0:T(2,128)} %param.11) | copy-start | bytes 76
  11.5 40.5 %collective-permute-start = (bf16[8,1,2,512]{3,0,2,1:T(8,128)(2,1)S(1)}, bf16[8,1,2,512]{3,0,2,1:T(8,128)(2,1)S(1)}, u32[]{:S(2)}, u32[]{:S(2)}) collective-permute-start(bf16[8,1,2,512]{3,0,2,1:T(8,128)(2,1)S(1)} %get-tuple-element.22), channel_id=1, source_target_pairs={{0,1},{1,2},{2,3},{4,5},{5,6},{6,7},{8,9},{9,10},{10,11},{12,13},{... | collective-permute-start | bytes 49160 | tf_op jit(solution)/shard_map/ppermute | solution.py:17
  13.9 38.1 %collective-permute-start.1 = (bf16[8,1,2,512]{3,0,2,1:T(8,128)(2,1)S(1)}, bf16[8,1,2,512]{3,0,2,1:T(8,128)(2,1)S(1)}, u32[]{:S(2)}, u32[]{:S(2)}) collective-permute-start(bf16[8,1,2,512]{3,0,2,1:T(8,128)(2,1)S(1)} %get-tuple-element.23), channel_id=1, source_target_pairs={{1,0},{2,1},{3,2},{5,4},{6,5},{7,6},{9,8},{10,9},{11,10},{13,12},{... | collective-permute-start | bytes 49160 | tf_op jit(solution)/shard_map/ppermute | solution.py:18
  68.5 4.2 %collective-permute-start.2 = (bf16[8,1,2,512]{3,0,2,1:T(8,128)(2,1)S(1)}, bf16[8,1,2,512]{3,0,2,1:T(8,128)(2,1)S(1)}, u32[]{:S(2)}, u32[]{:S(2)}) collective-permute-start(bf16[8,1,2,512]{3,0,2,1:T(8,128)(2,1)S(1)} %get-tuple-element.20), channel_id=1, source_target_pairs={{0,1},{1,2},{2,3},{4,5},{5,6},{6,7},{8,9},{9,10},{10,11},{12,13},{... | collective-permute-start | bytes 49160 | tf_op jit(solution)/shard_map/ppermute | solution.py:17
  70.8 4.6 %collective-permute-start.3 = (bf16[8,1,2,512]{3,0,2,1:T(8,128)(2,1)S(1)}, bf16[8,1,2,512]{3,0,2,1:T(8,128)(2,1)S(1)}, u32[]{:S(2)}, u32[]{:S(2)}) collective-permute-start(bf16[8,1,2,512]{3,0,2,1:T(8,128)(2,1)S(1)} %get-tuple-element.21), channel_id=1, source_target_pairs={{1,0},{2,1},{3,2},{5,4},{6,5},{7,6},{9,8},{10,9},{11,10},{13,12},{... | collective-permute-start | bytes 49160 | tf_op jit(solution)/shard_map/ppermute | solution.py:18
where the time goes:
time: 118 us
  blocking collectives  76.7 us (65%)
  other arithmetic  17.5 us (15%)
  local copies, waits for them, and re-layouts  8.32 us (7%)
  starting transfers between devices  7.2 us (6%)
  matrix products  4.26 us (4%)
  waiting for transfers between devices  2.63 us (2%)
    psum x1, blocking collectives, body(): summed = lax.psum(partial_grad, 'mode')  37.1 us
    all_gather x1, blocking collectives, body(): shard_rows = lax.all_gather(backward, 'mode', axis=0, tiled=True)  31.9 us
    psum x1, blocking collectives, body(): match_sum = lax.psum(block, 'row')  7.74 us
    ppermute x2, starting transfers between devices, padded_2(): before = lax.ppermute(last, axis, up)  4.61 us
    another operation x2, other arithmetic  3.81 us
    neg x1, other arithmetic, times_minus_i(): return jnp.stack([fields[:, :, 1], -fields[:, :, 0]], axis=2)  3.74 us
    slice x1, other arithmetic, times_minus_i(): return jnp.stack([fields[:, :, 1], -fields[:, :, 0]], axis=2)  3.74 us
    dot_general x2, matrix products, propagate(): jnp.dot(fields.reshape(-1, 2 * width), matrix, preferred_element_type=jnp...  2.92 us
  transfers between devices with their start and end apart: 4, of which 1 were waited for; matrix products, arithmetic and copies ran while one was open for 5% of the time, Pallas kernels for 0%

commit v1 on v0

--- a/solution.py
+++ b/solution.py
@@ -5,6 +5,24 @@
 from jax.sharding import PartitionSpec as P
 
 NG = 16
+
+
+def laid_out(blocks, dim):
+    blocks = jnp.moveaxis(blocks, 0, dim)
+    lengths = blocks.shape
+    return blocks.reshape(*lengths[:dim], lengths[dim] * lengths[dim + 1], *lengths[dim + 2 :])
+
+
+def grow_blocks(value, axis):
+    peers = lax.axis_size(axis)
+    blocks = value[None]
+    for level in range(peers.bit_length() - 1):
+        bit = 1 << level
+        theirs = lax.ppermute(blocks, axis, [(i, i ^ bit) for i in range(peers)])
+        both = jnp.stack([blocks, theirs])
+        upper = lax.axis_index(axis) >> level & 1
+        blocks = jnp.where(upper == 0, both, both[::-1]).reshape(-1, *value.shape)
+    return blocks
 
 
 def padded_2(array, sides, width):
@@ -115,7 +133,7 @@
     target_onehot = (target_groups[:, None] == group_ids[None, :]).astype(jnp.float32)
     own_pairs = jnp.dot(own_onehot, pair_matrix.T, precision=lax.Precision.HIGHEST)
     column_mask = jnp.dot(own_pairs, target_onehot.T, precision=lax.Precision.HIGHEST)
-    shard_rows = lax.all_gather(backward, "mode", axis=0, tiled=True)
+    shard_rows = laid_out(grow_blocks(backward, "mode"), 0)
     rows_flat = shard_rows.reshape(shard_rows.shape[0], -1)
     real_part = jnp.einsum("nd,kd->nk", field_flat, rows_flat, preferred_element_type=jnp.float32)
     imag_part = jnp.einsum("nd,kd->nk", field_turned, rows_flat, preferred_element_type=jnp.float32)

time: 118 us -> 128 us (1.085)
  waiting for transfers between devices: 2.63 us -> 7.51 us
  other arithmetic: 17.5 us -> 21.6 us
  blocking collectives: 76.7 us -> 73.9 us
  starting transfers between devices: 7.2 us -> 9.71 us
    ppermute x0 -> x3, waiting for transfers between devices: none -> 4.88 us  [grow_blocks(): theirs = lax.ppermute(blocks, axis, [(i, i ^ bit) for i in range(peers)])]
    ppermute x0 -> x3, starting transfers between devices: none -> 2.53 us  [grow_blocks(): theirs = lax.ppermute(blocks, axis, [(i, i ^ bit) for i in range(peers)])]
    another operation x2 -> x6, other arithmetic: 3.81 us -> 5.32 us
  transfers between devices with their start and end apart: 4 -> 7, of which waited for: 1 -> 3; matrix products, arithmetic and copies ran while one was open for 5% -> 12% of each run, Pallas kernels for 0% -> 0%
where the time goes in v1:
time: 128 us; the launch traced here: 127 us
  blocking collectives  73.9 us (58%)
  other arithmetic  21.6 us (17%)
  starting transfers between devices  9.71 us (8%)
  local copies, waits for them, and re-layouts  8.58 us (7%)
  waiting for transfers between devices  7.51 us (6%)
  matrix products  4.91 us (4%)
    psum x1, blocking collectives, body(): summed = lax.psum(partial_grad, 'mode')  36.1 us
    all_gather x1, blocking collectives, body(): shard_rows = lax.all_gather(backward, 'mode', axis=0, tiled=True)  31.2 us
    psum x1, blocking collectives, body(): match_sum = lax.psum(block, 'row')  6.63 us
    ppermute x3, waiting for transfers between devices, grow_blocks(): theirs = lax.ppermute(blocks, axis, [(i, i ^ bit) for i in range(peers)])  4.88 us
    ppermute x2, starting transfers between devices, padded_2(): before = lax.ppermute(last, axis, up)  4.6 us
    another operation x2, other arithmetic  3.83 us
    neg x1, other arithmetic, times_minus_i(): return jnp.stack([fields[:, :, 1], -fields[:, :, 0]], axis=2)  3.82 us
    slice x1, other arithmetic, times_minus_i(): return jnp.stack([fields[:, :, 1], -fields[:, :, 0]], axis=2)  3.82 us
  transfers between devices with their start and end apart: 7, of which 3 were waited for; matrix products, arithmetic and copies ran while one was open for 12% of the time, Pallas kernels for 0%

profile of v1, /device:TPU:0, one launch (start us, length us, event | category | flops | bytes accessed | tf_op | source)
XLA Modules:
  0.0 127.3 jit_solution(5459791669109771450)
XLA Ops:
  0.7 2.7 %slice_bitcast_fusion = (bf16[512,512]{0,1:T(8,128)(2,1)}, bf16[512,512]{0,1:T(8,128)(2,1)}, bf16[512,512]{1,0:T(8,128)(2,1)}, bf16[512,512]{1,0:T(8,128)(2,1)}) fusion(bf16[2,512,512]{2,1,0:T(8,128)(2,1)} %param.10), kind=kLoop, calls=%fused_computation.11 | loop fusion | bytes 3145728 | tf_op jit(solution)/shard_map/transpose | solution.py:68
  3.4 0.8 fusion.13
  4.3 0.3 fusion.20
  4.7 1.8 %maximum_bitcast_fusion = bf16[1024,1024]{0,1:T(8,128)(2,1)S(1)} fusion(bf16[512,512]{1,0:T(8,128)(2,1)} %get-tuple-element.13, bf16[512,512]{1,0:T(8,128)(2,1)} %fusion.13, bf16[512,512]{1,0:T(8,128)(2,1)} %get-tuple-element.12), kind=kLoop, calls=%fused_computation.3 | loop fusion | flops 8388608 | bytes 3670016 | tf_op jit(solution)/shard_map/dot_general | solution.py:75
  6.5 2.6 %copy.22 = bf16[1024,1024]{1,0:T(8,128)(2,1)} copy(bf16[1024,1024]{0,1:T(8,128)(2,1)S(1)} %maximum_bitcast_fusion) | data formatting | bytes 4194304 | tf_op jit(solution)/shard_map/dot_general | solution.py:75
  9.1 2.3 %convolution_convert_fusion = bf16[8,2,2,512]{3,0,2,1:T(8,128)(2,1)S(1)} fusion(bf16[8,2,1024,1]{2,0,3,1:T(8,128)(2,1)S(1)} %bitcast.104, bf16[2,512,1024,1]{2,1,0,3:T(8,128)(2,1)} %bitcast.99), kind=kOutput, calls=%fused_computation.5 | convolution fusion | flops 33570816 | bytes 2162688 | tf_op jit(solution)/shard_map/dot_general | solution.py:75
  11.4 0.6 fusion.18
  12.0 2.3 %collective-permute-start = (bf16[8,1,2,512]{3,0,2,1:T(8,128)(2,1)}, bf16[8,1,2,512]{3,0,2,1:T(8,128)(2,1)S(1)}, u32[]{:S(2)}, u32[]{:S(2)}) collective-permute-start(bf16[8,1,2,512]{3,0,2,1:T(8,128)(2,1)} %get-tuple-element.24), channel_id=1, source_target_pairs={{0,1},{1,2},{2,3},{4,5},{5,6},{6,7},{8,9},{9,10},{10,11},{12,13},{... | collective-permute-start | bytes 49160 | tf_op jit(solution)/shard_map/ppermute | solution.py:35
  14.4 1.3 %collective-permute-start.1 = (bf16[8,1,2,512]{3,0,2,1:T(8,128)(2,1)}, bf16[8,1,2,512]{3,0,2,1:T(8,128)(2,1)}, u32[]{:S(2)}, u32[]{:S(2)}) collective-permute-start(bf16[8,1,2,512]{3,0,2,1:T(8,128)(2,1)} %get-tuple-element.25), channel_id=1, source_target_pairs={{1,0},{2,1},{3,2},{5,4},{6,5},{7,6},{9,8},{10,9},{11,10},{13,12},{... | collective-permute-start | bytes 49160 | tf_op jit(solution)/shard_map/ppermute | solution.py:36
  15.7 2.4 %collective-permute-start.2 = (bf16[1,8,2,2,512]{4,3,2,1,0:T(2,128)(2,1)S(1)}, bf16[1,8,2,2,512]{4,3,2,1,0:T(2,128)(2,1)}, u32[]{:S(2)}, u32[]{:S(2)}) collective-permute-start(bf16[1,8,2,2,512]{4,3,2,1,0:T(2,128)(2,1)S(1)} %bitcast.109), channel_id=1, source_target_pairs={{0,4},{4,0},{8,12},{12,8},{16,20},{20,16},{24,28},{28,24},{1,5},{5... | collective-permute-start | bytes 98312 | tf_op jit(solution)/shard_map/ppermute | solution.py:21
  18.1 31.2 %all_gather.3 = bf16[64,2,2,512]{3,2,1,0:T(2,128)(2,1)S(1)} all-gather(bf16[8,2,2,512]{3,2,1,0:T(2,128)(2,1)S(1)} %copy-done.4), channel_id=1, replica_groups=mesh['mode'=8,'row'=4] {'mode'}, dimensions={0}, use_global_device_ids=true | all-gather | bytes 294912 | tf_op jit(solution)/shard_map/all_gather | solution.py:144
  49.2 0.8 fusion.14
  50.1 0.6 slice_negate_fusion
  50.7 0.5 slice_negate_fusion.1
  51.3 0.1 convert_reduce_fusion
  51.4 0.2 fusion.5
  51.6 0.8 convolution_multiply_fusion.1
  52.4 0.6 pad_maximum_fusion.1
  53.0 1.6 %maximum_maximum_fusion = bf16[1024,1024]{0,1:T(8,128)(2,1)S(1)} fusion(bf16[512,512]{0,1:T(8,128)(2,1)} %get-tuple-element.11, bf16[512,512]{0,1:T(8,128)(2,1)} %get-tuple-element.10, bf16[512,512]{0,1:T(8,128)(2,1)S(1)} %copy-done.2), kind=kLoop, calls=%fused_computation.4 | loop fusion | flops 8388608 | bytes 3670016 | tf_op jit(solution)/shard_map/concatenate | solution.py:70
  54.6 0.7 fusion.21
  55.3 0.2 reshape.187
  55.5 0.2 reshape.188
  55.7 0.7 maximum_convert_fusion
  56.5 0.9 pad_maximum_fusion.3
  57.3 0.1 fusion.7
  57.5 3.8 %fusion.16 = (bf16[8,2,1,512]{3,0,2,1:T(8,128)(2,1)S(1)}, bf16[8,2,1,512]{3,0,2,1:T(8,128)(2,1)S(1)}) fusion(f32[8,4,2,512]{3,0,2,1:T(8,128)S(1)} %maximum_convert_fusion, f32[]{:T(128)} %bitcast.16, f32[]{:T(128)} %bitcast.15, f32[]{:T(128)} %bitcast.14, f32[]{:T(128)} %bitcast.13, f32[]{:T(128)} %bitcast.12, f32[]{:T(128)} %bitcast), kind=kLoop, calls=%fused_computation.72 | loop fusion | flops 106496 | bytes 229400 | tf_op jit(solution)/shard_map/neg | solution.py:109
  61.3 1.6 %collective-permute-done.3 = bf16[2,8,2,2,512]{4,3,2,1,0:T(2,128)(2,1)S(1)} collective-permute-done((bf16[2,8,2,2,512]{4,3,2,1,0:T(2,128)(2,1)S(1)}, bf16[2,8,2,2,512]{4,3,2,1,0:T(2,128)(2,1)S(1)}, u32[]{:S(2)}, u32[]{:S(2)}) %collective-permute-start.3) | collective-permute-done | bytes 65568 | tf_op jit(solution)/shard_map/ppermute | solution.py:21
  63.0 0.2 pad_maximum_fusion.2
  63.2 0.1 broadcast_select_fusion.1
  63.4 3.8 %add_convert_fusion.1 = bf16[8,2,1,512]{3,0,2,1:T(8,128)(2,1)S(1)} fusion(f32[8,4,2,512]{3,0,2,1:T(8,128)S(1)} %maximum_convert_fusion, f32[]{:T(128)} %bitcast.16, f32[]{:T(128)} %bitcast.15, f32[]{:T(128)} %bitcast.14, f32[]{:T(128)} %bitcast.13, f32[]{:T(128)} %bitcast.12, f32[]{:T(128)} %bitcast), kind=kLoop, calls=%fused_computation.35 | loop fusion | flops 98304 | bytes 213016 | tf_op jit(solution)/shard_map/slice | solution.py:109
  67.2 3.2 %collective-permute-done.4 = bf16[4,8,2,2,512]{4,3,2,1,0:T(2,128)(2,1)S(1)} collective-permute-done((bf16[4,8,2,2,512]{4,3,2,1,0:T(2,128)(2,1)S(1)}, bf16[4,8,2,2,512]{4,3,2,1,0:T(2,128)(2,1)S(1)}, u32[]{:S(2)}, u32[]{:S(2)}) %collective-permute-start.4) | collective-permute-done | bytes 131104 | tf_op jit(solution)/shard_map/ppermute | solution.py:21
  70.4 0.4 pad_maximum_fusion
  70.8 0.2 broadcast_select_fusion
  71.1 0.2 reshape_reshape_reshape.3
  71.2 0.2 convolution_bitcast_fusion.1
  71.4 0.2 convolution_bitcast_fusion
  71.6 6.6 %psum.14 = f32[2,8,64]{2,1,0:T(8,128)S(1)} all-reduce(f32[2,8,64]{2,1,0:T(8,128)S(1)} %pad_maximum_fusion.7), channel_id=1, replica_groups=mesh['mode'=8,'row'=4] {'row'}, use_global_device_ids=true, to_apply=%region_0.0 | all-reduce | flops 1024 | bytes 8192 | tf_op jit(solution)/shard_map/psum | solution.py:141
  78.3 0.6 fusion.15
  78.9 0.1 fusion.8
  79.0 0.2 fusion.1
  79.2 2.3 %collective-permute-start.5 = (bf16[8,1,2,512]{3,0,2,1:T(8,128)(2,1)S(1)}, bf16[8,1,2,512]{3,0,2,1:T(8,128)(2,1)S(1)}, u32[]{:S(2)}, u32[]{:S(2)}) collective-permute-start(bf16[8,1,2,512]{3,0,2,1:T(8,128)(2,1)S(1)} %get-tuple-element.22), channel_id=1, source_target_pairs={{0,1},{1,2},{2,3},{4,5},{5,6},{6,7},{8,9},{9,10},{10,11},{12,13},{... | collective-permute-start | bytes 49160 | tf_op jit(solution)/shard_map/ppermute | solution.py:35
  81.4 1.3 %collective-permute-start.6 = (bf16[8,1,2,512]{3,0,2,1:T(8,128)(2,1)S(1)}, bf16[8,1,2,512]{3,0,2,1:T(8,128)(2,1)S(1)}, u32[]{:S(2)}, u32[]{:S(2)}) collective-permute-start(bf16[8,1,2,512]{3,0,2,1:T(8,128)(2,1)S(1)} %get-tuple-element.23), channel_id=1, source_target_pairs={{1,0},{2,1},{3,2},{5,4},{6,5},{7,6},{9,8},{10,9},{11,10},{13,12},{... | collective-permute-start | bytes 49160 | tf_op jit(solution)/shard_map/ppermute | solution.py:36
  82.7 0.7 fusion.22
  83.4 2.6 %collective-permute-done.6 = bf16[8,1,2,512]{3,0,2,1:T(8,128)(2,1)S(1)} collective-permute-done((bf16[8,1,2,512]{3,0,2,1:T(8,128)(2,1)S(1)}, bf16[8,1,2,512]{3,0,2,1:T(8,128)(2,1)S(1)}, u32[]{:S(2)}, u32[]{:S(2)}) %collective-permute-start.6) | collective-permute-done | bytes 16416 | tf_op jit(solution)/shard_map/ppermute | solution.py:36
  86.1 3.8 %subtract_convert_fusion = (bf16[8,2,1,512]{3,0,2,1:T(8,128)(2,1)S(1)}, bf16[8,2,1,512]{3,0,2,1:T(8,128)(2,1)S(1)}) fusion(f32[8,4,2,512]{3,0,2,1:T(8,128)S(1)} %maximum_convert_fusion.1, f32[]{:T(128)} %bitcast.37, f32[]{:T(128)} %bitcast.36, f32[]{:T(128)} %bitcast.35, f32[]{:T(128)} %bitcast.15, f32[]{:T(128)} %bitcast.13, f32[]{:T(128)} %bitcast), kind=kLoop, calls=%fused_computation.33 | loop fusion | flops 196608 | bytes 229400 | tf_op jit(solution)/shard_map/convert.1
  89.9 0.6 fusion.23
  90.6 36.1 %psum.15 = f32[4,2,512]{2,0,1:T(4,128)S(1)} all-reduce(f32[4,2,512]{2,0,1:T(4,128)S(1)} %reduce_sum.19), channel_id=1, replica_groups=mesh['mode'=8,'row'=4] {'mode'}, use_global_device_ids=true, to_apply=%region_3.4 | all-reduce | flops 4096 | bytes 32768 | tf_op jit(solution)/shard_map/psum | solution.py:163
  126.7 0.6 copy.23
  (48 shorter events, 0.4 us)
Async XLA Ops:
  0.6 3.7 %copy-start = (f32[7,2,512]{2,1,0:T(2,128)S(1)}, f32[7,2,512]{2,1,0:T(2,128)}, u32[]{:S(2)}) copy-start(f32[7,2,512]{2,1,0:T(2,128)} %param.12) | copy-start | bytes 86020
  0.6 2.8 %copy-start.1 = (bf16[2,512,512]{2,1,0:T(8,128)(2,1)S(1)}, bf16[2,512,512]{2,1,0:T(8,128)(2,1)}, u32[]{:S(2)}) copy-start(bf16[2,512,512]{2,1,0:T(8,128)(2,1)} %param.10) | copy-start | bytes 3145732
  0.7 3.6 %copy-start.3 = (bf16[8,2,2,512]{3,2,1,0:T(2,128)(2,1)S(1)}, bf16[8,2,2,512]{3,2,1,0:T(2,128)(2,1)}, u32[]{:S(2)}) copy-start(bf16[8,2,2,512]{3,2,1,0:T(2,128)(2,1)} %param.8) | copy-start | bytes 98308
  0.7 3.6 %copy-start.10 = (s32[4]{0:T(128)S(1)}, s32[4]{0:T(128)}, u32[]{:S(2)}) copy-start(s32[4]{0:T(128)} %param.13) | copy-start | bytes 52
  0.7 3.6 %copy-start.9 = (f32[4]{0:T(128)S(1)}, f32[4]{0:T(128)}, u32[]{:S(2)}) copy-start(f32[4]{0:T(128)} %param.14) | copy-start | bytes 52
  9.1 6.6 %copy-start.4 = (bf16[8,2,2,512]{3,2,1,0:T(2,128)(2,1)S(1)}, bf16[8,2,2,512]{3,2,1,0:T(2,128)(2,1)}, u32[]{:S(2)}) copy-start(bf16[8,2,2,512]{3,2,1,0:T(2,128)(2,1)} %param.9) | copy-start | bytes 98308
  9.1 41.0 %copy-start.8 = (s32[80,2]{0,1:T(2,128)S(1)}, s32[80,2]{0,1:T(2,128)}, u32[]{:S(2)}) copy-start(s32[80,2]{0,1:T(2,128)} %param.15) | copy-start | bytes 1924
  9.1 41.6 %copy-start.5 = (f32[2,3]{1,0:T(2,128)S(1)}, f32[2,3]{1,0:T(2,128)}, u32[]{:S(2)}) copy-start(f32[2,3]{1,0:T(2,128)} %param.11) | copy-start | bytes 76
  12.0 43.7 %collective-permute-start = (bf16[8,1,2,512]{3,0,2,1:T(8,128)(2,1)}, bf16[8,1,2,512]{3,0,2,1:T(8,128)(2,1)S(1)}, u32[]{:S(2)}, u32[]{:S(2)}) collective-permute-start(bf16[8,1,2,512]{3,0,2,1:T(8,128)(2,1)} %get-tuple-element.24), channel_id=1, source_target_pairs={{0,1},{1,2},{2,3},{4,5},{5,6},{6,7},{8,9},{9,10},{10,11},{12,13},{... | collective-permute-start | bytes 49160 | tf_op jit(solution)/shard_map/ppermute | solution.py:35
  14.4 41.3 %collective-permute-start.1 = (bf16[8,1,2,512]{3,0,2,1:T(8,128)(2,1)}, bf16[8,1,2,512]{3,0,2,1:T(8,128)(2,1)}, u32[]{:S(2)}, u32[]{:S(2)}) collective-permute-start(bf16[8,1,2,512]{3,0,2,1:T(8,128)(2,1)} %get-tuple-element.25), channel_id=1, source_target_pairs={{1,0},{2,1},{3,2},{5,4},{6,5},{7,6},{9,8},{10,9},{11,10},{13,12},{... | collective-permute-start | bytes 49160 | tf_op jit(solution)/shard_map/ppermute | solution.py:36
  15.7 40.8 %collective-permute-start.2 = (bf16[1,8,2,2,512]{4,3,2,1,0:T(2,128)(2,1)S(1)}, bf16[1,8,2,2,512]{4,3,2,1,0:T(2,128)(2,1)}, u32[]{:S(2)}, u32[]{:S(2)}) collective-permute-start(bf16[1,8,2,2,512]{4,3,2,1,0:T(2,128)(2,1)S(1)} %bitcast.109), channel_id=1, source_target_pairs={{0,4},{4,0},{8,12},{12,8},{16,20},{20,16},{24,28},{28,24},{1,5},{5... | collective-permute-start | bytes 98312 | tf_op jit(solution)/shard_map/ppermute | solution.py:21
  50.1 2.9 %copy-start.2 = (bf16[512,512]{0,1:T(8,128)(2,1)S(1)}, bf16[512,512]{0,1:T(8,128)(2,1)}, u32[]{:S(2)}) copy-start(bf16[512,512]{0,1:T(8,128)(2,1)} %fusion.14) | copy-start | bytes 1572868
  55.5 22.7 %copy-start.7 = (f32[8,64]{1,0:T(8,128)S(1)}, f32[8,64]{1,0:T(8,128)}, u32[]{:S(2)}) copy-start(f32[8,64]{1,0:T(8,128)} %convolution_multiply_fusion.1) | copy-start | bytes 6148
  57.4 25.3 %copy-start.6 = (f32[1,3]{1,0:T(1,128)S(1)}, f32[1,3]{1,0:T(1,128)}, u32[]{:S(2)}) copy-start(f32[1,3]{1,0:T(1,128)} %slice_negate_fusion.1) | copy-start | bytes 40
  57.4 5.6 %collective-permute-start.3 = (bf16[2,8,2,2,512]{4,3,2,1,0:T(2,128)(2,1)S(1)}, bf16[2,8,2,2,512]{4,3,2,1,0:T(2,128)(2,1)S(1)}, u32[]{:S(2)}, u32[]{:S(2)}) collective-permute-start(bf16[2,8,2,2,512]{4,3,2,1,0:T(2,128)(2,1)S(1)} %get-tuple-element.21), channel_id=1, source_target_pairs={{0,8},{4,12},{8,0},{12,4},{16,24},{20,28},{24,16},{28,20},{1,9},{5... | collective-permute-start | bytes 196616 | tf_op jit(solution)/shard_map/ppermute | solution.py:21
  63.3 7.2 %collective-permute-start.4 = (bf16[4,8,2,2,512]{4,3,2,1,0:T(2,128)(2,1)S(1)}, bf16[4,8,2,2,512]{4,3,2,1,0:T(2,128)(2,1)S(1)}, u32[]{:S(2)}, u32[]{:S(2)}) collective-permute-start(bf16[4,8,2,2,512]{4,3,2,1,0:T(2,128)(2,1)S(1)} %bitcast.100), channel_id=1, source_target_pairs={{0,16},{4,20},{8,24},{12,28},{16,0},{20,4},{24,8},{28,12},{1,17},{... | collective-permute-start | bytes 393224 | tf_op jit(solution)/shard_map/ppermute | solution.py:21
  79.2 4.2 %collective-permute-start.5 = (bf16[8,1,2,512]{3,0,2,1:T(8,128)(2,1)S(1)}, bf16[8,1,2,512]{3,0,2,1:T(8,128)(2,1)S(1)}, u32[]{:S(2)}, u32[]{:S(2)}) collective-permute-start(bf16[8,1,2,512]{3,0,2,1:T(8,128)(2,1)S(1)} %get-tuple-element.22), channel_id=1, source_target_pairs={{0,1},{1,2},{2,3},{4,5},{5,6},{6,7},{8,9},{9,10},{10,11},{12,13},{... | collective-permute-start | bytes 49160 | tf_op jit(solution)/shard_map/ppermute | solution.py:35
  81.4 4.6 %collective-permute-start.6 = (bf16[8,1,2,512]{3,0,2,1:T(8,128)(2,1)S(1)}, bf16[8,1,2,512]{3,0,2,1:T(8,128)(2,1)S(1)}, u32[]{:S(2)}, u32[]{:S(2)}) collective-permute-start(bf16[8,1,2,512]{3,0,2,1:T(8,128)(2,1)S(1)} %get-tuple-element.23), channel_id=1, source_target_pairs={{1,0},{2,1},{3,2},{5,4},{6,5},{7,6},{9,8},{10,9},{11,10},{13,12},{... | collective-permute-start | bytes 49160 | tf_op jit(solution)/shard_map/ppermute | solution.py:36
